TPU v7x, 512 devices: a whole 4x8x8 slice. The times are simulated.
512 devices in a mesh: region: 32 (over x, z), tm: 16 (over y, core).
Axes of the slice: x: 4, y: 8, z: 8, core: 2. Of those that a mesh axis runs over, the one named last changes fastest.
Arguments:
- right_side: float32 [1024, 65536], P('tm', 'region'), may hold values from -9 to 9
- initial: float32 [1024, 65536], P('tm', 'region'), may hold values from -1.5 to 1.5
- blocks: bfloat16 [512, 9, 128, 128], P(('region', 'tm')), may hold values from -2.5 to 3.1, as said below
- neighbour_blocks: int32 [512, 8], P('region'), may hold values from 0 to 511, as said below
- temporal_cov: bfloat16 [1024, 1024], P('tm'), may hold values from -2.5 to 2.8, as said below
Outputs:
- solution: float32 [1024, 65536], P('tm', 'region')
- residual: float32 [1024, 65536], P('tm', 'region')
Inputs may be any that keep to these rules, and one draw needn't show every extreme that they name: blocks[i, 0] is symmetric positive definite. `neighbour_blocks`: each column names every block exactly once. Blocks fall into cyclic windows of 16 consecutive blocks starting at 8 + m * 16, and every block listed for row i lies in the window of i. temporal_cov is symmetric positive definite.
All inputs are finite; a program needn't handle non-finite values.
Results may differ from a plain program's by a relative error of at most 0.012.
The roundings to bfloat16 on the way count: a program that leaves them out, or rounds other values in their place, can miss the bound.
Values may be sent and summed in bfloat16 or wider, within the bound.
No kernel may reach another device: no remote copies, remote signals or barrier semaphores. Data moves between devices by JAX's collectives and lax.ppermute only.
A program may use at most 64 MiB of HBM per device.

v0:
```python
import jax
import jax.numpy as jnp
from jax import lax
from jax.sharding import Mesh
from jax.sharding import PartitionSpec as P

ITERS = 2
REGION = ("region_0", "region_1")
TM = ("tm_0", "tm_1")
REGION_TM = ("region_0", "region_1", "tm_0", "tm_1")


def with_halo(value, sides, width):
    for axis, dim in sides:
        peers, length = (lax.axis_size(axis), value.shape[dim])
        up = [(i, (i + 1) % peers) for i in range(peers)]
        down = [(j, i) for i, j in up]
        last = lax.slice_in_dim(value, length - width, length, axis=dim)
        initial = lax.slice_in_dim(value, 0, width, axis=dim)
        before = lax.ppermute(last, axis, up)
        after = lax.ppermute(initial, axis, down)
        value = jnp.concatenate([before, value, after], axis=dim)
    return value


def gather_axes(value, axes, dim):
    for axis in reversed(axes):
        value = lax.all_gather(value, axis, axis=dim, tiled=True)
    return value


def one_axis_at_a_time(value, axes):
    for axis in axes:
        value = lax.psum(value, axis)
    return value


def local_tiles(lowered, neighbour_blocks):
    row_count = neighbour_blocks.shape[0]
    tile_width = lowered.shape[1] // row_count
    widened = with_halo(lowered, ((REGION, 1),), row_count // 2 * tile_width)
    region = lax.axis_index(REGION)
    block_total = row_count * lax.axis_size(REGION)
    offset = jnp.mod(neighbour_blocks - region * row_count + row_count // 2, block_total)
    itself = (jnp.arange(row_count, dtype=jnp.int32) + row_count // 2)[:, None]
    places = jnp.concatenate([itself, offset], axis=1)
    cell_tiles = widened.reshape(widened.shape[0], 2 * row_count, tile_width)
    return jnp.take(cell_tiles, places, axis=1)


def local(right_side, initial, blocks, neighbour_blocks, temporal_cov):
    hour_matrix = gather_axes(temporal_cov, TM, 0)
    region_blocks = lax.all_gather(blocks, TM, axis=0, tiled=True)
    tm_count = lax.axis_size(TM)
    hour_slice = right_side.shape[0]
    site_count = right_side.shape[1]
    tile_width = blocks.shape[2]
    own_rows = blocks.shape[0]

    def temporal(arrived):
        item_count = arrived.shape[2]
        flattened = arrived.reshape(arrived.shape[0], item_count * tile_width)
        blended = jnp.dot(hour_matrix, flattened, preferred_element_type=jnp.float32).astype(
            jnp.bfloat16
        )
        return blended.reshape(arrived.shape[0], 1, item_count, tile_width)

    def operate(current):
        lowered = current.astype(jnp.bfloat16)
        tile_stack = local_tiles(lowered, neighbour_blocks)
        spatial = jnp.einsum(
            "hrkb,rkab->hra", tile_stack, region_blocks, preferred_element_type=jnp.float32
        )
        spatial = spatial.astype(jnp.bfloat16).reshape(hour_slice, tm_count, own_rows, tile_width)
        blended = temporal(lax.all_to_all(spatial, TM, split_axis=1, concat_axis=0, tiled=True))
        returned = lax.all_to_all(blended, TM, split_axis=0, concat_axis=1, tiled=True)
        return current + returned.reshape(hour_slice, site_count).astype(jnp.float32)

    solution = initial
    residual = right_side - operate(initial)
    direction = residual
    norm_now = one_axis_at_a_time(jnp.sum(residual * residual), REGION_TM)
    for iteration in range(ITERS):
        applied = operate(direction)
        curvature, cross_term, square = (
            one_axis_at_a_time(jnp.sum(direction * applied), REGION_TM),
            one_axis_at_a_time(jnp.sum(residual * applied), REGION_TM),
            one_axis_at_a_time(jnp.sum(applied * applied), REGION_TM),
        )
        step_size = norm_now / curvature
        solution = solution + step_size * direction
        norm_next = norm_now - 2.0 * step_size * cross_term + step_size * step_size * square
        residual = residual - step_size * applied
        if iteration + 1 < ITERS:
            direction = residual + norm_next / norm_now * direction
        norm_now = norm_next
    return (solution, residual)


def solution(mesh):
    split = Mesh(mesh.devices.reshape(4, 8, 8, 2), ("region_0", "region_1", "tm_0", "tm_1"))
    return jax.shard_map(
        local,
        mesh=split,
        in_specs=(
            P(TM, REGION),
            P(TM, REGION),
            P(REGION_TM, None, None, None),
            P(REGION, None),
            P(TM, None),
        ),
        out_specs=(P(TM, REGION), P(TM, REGION)),
        check_vma=False,
    )
```

profile of v0, /device:TPU:1, one launch (start us, length us, event | category | flops | bytes accessed | tf_op | source)
XLA Modules:
  0.0 342.4 jit_solution(12038400127978279072)
XLA Ops:
  7.2 0.7 all-gather.3.cloned.1.call-update
  7.9 10.2 %all_gather.10 = bf16[128,1024]{1,0:T(8,128)(2,1)} all-gather(bf16[64,1024]{1,0:T(8,128)(2,1)} %param.11), channel_id=1, replica_groups=mesh['region_0'=4,'region_1'=8,'tm_0'=8,'tm_1'=2] {'tm_1'}, dimensions={0}, use_global_device_ids=true | all-gather | bytes 393216 | tf_op jit(solution)/shard_map/all_gather | solution.py:28
  18.2 1.1 convert_element_type.81
  19.3 1.9 collective-permute-start
  21.2 7.5 %collective-permute-start.1 = (bf16[64,1024]{1,0:T(8,128)(2,1)S(1)}, bf16[64,1024]{1,0:T(8,128)(2,1)S(1)}, u32[]{:S(2)}, u32[]{:S(2)}) collective-permute-start(bf16[64,1024]{1,0:T(8,128)(2,1)S(1)} %get-tuple-element.27), channel_id=1, source_target_pairs={{16,0},{32,16},{48,32},{64,48},{80,64},{96,80},{112,96},{128,112},... | collective-permute-start | bytes 393224 | tf_op jit(solution)/shard_map/ppermute | solution.py:21
  28.8 0.7 add_select_fusion
  29.8 0.8 collective-permute-done
  30.5 0.9 collective-permute-done.1
  31.6 1.0 gather_fusion
  32.6 27.8 %all-gather.3.cloned.1.call-done = bf16[16,9,128,128]{3,2,1,0:T(8,128)(2,1)} async-done(((bf16[1,9,128,128]{3,2,1,0:T(8,128)(2,1)}), bf16[16,9,128,128]{3,2,1,0:T(8,128)(2,1)}) %all-gather.3.cloned.1.call-update) | async-done | bytes 4718608 | tf_op jit(solution)/shard_map/all_gather | solution.py:53
  60.5 5.0 %fusion.36 = bf16[64,16,1,128]{3,0,2,1:T(8,128)(2,1)} fusion(bf16[16,9,128,128]{3,2,1,0:T(8,128)(2,1)} %all-gather.3.cloned.1.call-done, bf16[16,9,64,128]{3,2,1,0:T(8,128)(2,1)S(1)} %bitcast.174, pred[16,9]{1,0:T(8,128)(4,1)S(1)} %copy.40), kind=kOutput, calls=%fused_computation.30 | convolution fusion | flops 303300608 | bytes 7340176 | tf_op jit(solution)/shard_map/hrkb,rkab->hra/dot_general | solution.py:71
  65.5 5.0 %all-to-all-start = ((bf16[64,16,1,128]{3,0,2,1:T(8,128)(2,1)}), bf16[64,16,1,128]{3,0,2,1:T(8,128)(2,1)S(1)}, u32[]{:S(2)}, u32[]{:S(2)}) async-start(bf16[64,16,1,128]{3,0,2,1:T(8,128)(2,1)} %fusion.36), calls=%async_computation | async-start | bytes 524288 | tf_op jit(solution)/shard_map/all_to_all | solution.py:75
  70.5 31.9 %all-gather.5.cloned.1.call-done = bf16[1024,1024]{1,0:T(8,128)(2,1)} async-done(((bf16[128,1024]{1,0:T(8,128)(2,1)}), bf16[1024,1024]{1,0:T(8,128)(2,1)}) %all-gather.5.cloned.1.call-update) | async-done | bytes 2097168 | tf_op jit(solution)/shard_map/all_gather | solution.py:28
  102.3 2.4 fusion.33
  104.7 0.5 broadcast.101
  105.3 0.8 reduce
  106.3 20.0 %all_to_all.72 = bf16[16,2,4096]{2,1,0:T(2,128)(2,1)S(1)} all-to-all(bf16[16,2,4096]{2,1,0:T(2,128)(2,1)S(1)} %reshape.136), channel_id=1, replica_groups=mesh['region_0'=4,'region_1'=8,'tm_0'=8,'tm_1'=2] {'tm_0','tm_1'}, dimensions={0} | all-to-all | bytes 524288 | tf_op jit(solution)/shard_map/all_to_all | solution.py:76
  127.3 3.3 collective-permute-start.2
  130.6 6.4 %collective-permute-start.3 = (bf16[64,1024]{1,0:T(8,128)(2,1)S(1)}, bf16[64,1024]{1,0:T(8,128)(2,1)S(1)}, u32[]{:S(2)}, u32[]{:S(2)}) collective-permute-start(bf16[64,1024]{1,0:T(8,128)(2,1)S(1)} %get-tuple-element.25), channel_id=1, source_target_pairs={{16,0},{32,16},{48,32},{64,48},{80,64},{96,80},{112,96},{128,112},... | collective-permute-start | bytes 393224 | tf_op jit(solution)/shard_map/ppermute | solution.py:21
  136.9 1.8 collective-permute-done.2
  138.7 1.4 collective-permute-done.3
  140.3 2.5 gather_fusion.1
  142.7 5.1 %fusion.39 = bf16[64,16,1,128]{3,0,2,1:T(8,128)(2,1)S(1)} fusion(bf16[16,9,128,128]{3,2,1,0:T(8,128)(2,1)} %all-gather.3.cloned.1.call-done, bf16[16,9,64,128]{3,2,1,0:T(8,128)(2,1)} %bitcast.176, pred[16,9]{1,0:T(8,128)(4,1)S(1)} %copy.40), kind=kOutput, calls=%fused_computation.31 | convolution fusion | flops 303300608 | bytes 7340176 | tf_op jit(solution)/shard_map/hrkb,rkab->hra/dot_general | solution.py:71
  147.9 14.7 %all_to_all.73 = bf16[64,16,1,128]{3,0,2,1:T(8,128)(2,1)S(1)} all-to-all(bf16[64,16,1,128]{3,0,2,1:T(8,128)(2,1)S(1)} %fusion.39), channel_id=1, replica_groups=mesh['region_0'=4,'region_1'=8,'tm_0'=8,'tm_1'=2] {'tm_0','tm_1'}, dimensions={1} | all-to-all | bytes 524288 | tf_op jit(solution)/shard_map/all_to_all | solution.py:75
  162.6 0.8 fusion.34
  163.4 0.8 reduce.1
  164.5 14.2 %all_to_all.74 = bf16[16,2,4096]{2,1,0:T(2,128)(2,1)S(1)} all-to-all(bf16[16,2,4096]{2,1,0:T(2,128)(2,1)S(1)} %reshape.138), channel_id=1, replica_groups=mesh['region_0'=4,'region_1'=8,'tm_0'=8,'tm_1'=2] {'tm_0','tm_1'}, dimensions={0} | all-to-all | bytes 524288 | tf_op jit(solution)/shard_map/all_to_all | solution.py:76
  179.4 0.9 multiply_reduce_fusion.1
  180.3 7.2 %all-reduce.2 = (f32[]{:T(128)}, f32[]{:T(128)}, f32[]{:T(128)}) all-reduce(f32[]{:T(128)} %get-tuple-element.5, f32[]{:T(128)} %get-tuple-element.4, f32[]{:T(128)} %get-tuple-element.3), channel_id=1, replica_groups=mesh['region_0'=4,'region_1'=8,'tm_0'=8,'tm_1'=2] {'region_0'}, use_global_device_ids=true, to_apply=%region_1.3 | all-reduce | flops 3 | bytes 24 | tf_op jit(solution)/shard_map/psum | solution.py:34
  187.5 16.8 %all-reduce.1 = (f32[]{:T(128)}, f32[]{:T(128)}, f32[]{:T(128)}) all-reduce(f32[]{:T(128)} %get-tuple-element.12, f32[]{:T(128)} %get-tuple-element.13, f32[]{:T(128)} %get-tuple-element.14), channel_id=1, replica_groups=mesh['region_0'=4,'region_1'=8,'tm_0'=8,'tm_1'=2] {'region_1'}, use_global_device_ids=true, to_apply=%region_2.4 | all-reduce | flops 3 | bytes 24 | tf_op jit(solution)/shard_map/psum | solution.py:34
  204.3 11.7 %all-reduce = (f32[]{:T(128)}, f32[]{:T(128)}, f32[]{:T(128)}) all-reduce(f32[]{:T(128)} %get-tuple-element.9, f32[]{:T(128)} %get-tuple-element.10, f32[]{:T(128)} %get-tuple-element.11), channel_id=1, replica_groups=mesh['region_0'=4,'region_1'=8,'tm_0'=8,'tm_1'=2] {'tm_0'}, use_global_device_ids=true, to_apply=%region_3.5 | all-reduce | flops 3 | bytes 24 | tf_op jit(solution)/shard_map/psum | solution.py:34
  216.0 11.5 %all-reduce.3 = (f32[]{:T(128)}, f32[]{:T(128)}, f32[]{:T(128)}) all-reduce(f32[]{:T(128)} %get-tuple-element.6, f32[]{:T(128)} %get-tuple-element.7, f32[]{:T(128)} %get-tuple-element.8), channel_id=1, replica_groups=mesh['region_0'=4,'region_1'=8,'tm_0'=8,'tm_1'=2] {'tm_1'}, use_global_device_ids=true, to_apply=%region_4.6 | all-reduce | flops 3 | bytes 24 | tf_op jit(solution)/shard_map/psum | solution.py:34
  231.4 1.9 collective-permute-start.4
  233.3 6.7 %collective-permute-start.5 = (bf16[64,1024]{1,0:T(8,128)(2,1)S(1)}, bf16[64,1024]{1,0:T(8,128)(2,1)S(1)}, u32[]{:S(2)}, u32[]{:S(2)}) collective-permute-start(bf16[64,1024]{1,0:T(8,128)(2,1)S(1)} %get-tuple-element.23), channel_id=1, source_target_pairs={{16,0},{32,16},{48,32},{64,48},{80,64},{96,80},{112,96},{128,112},... | collective-permute-start | bytes 393224 | tf_op jit(solution)/shard_map/ppermute | solution.py:21
  240.0 1.3 collective-permute-done.4
  241.3 0.9 collective-permute-done.5
  242.4 2.5 gather_fusion.2
  244.9 5.0 %fusion.42 = bf16[64,16,1,128]{3,0,2,1:T(8,128)(2,1)S(1)} fusion(bf16[16,9,128,128]{3,2,1,0:T(8,128)(2,1)} %all-gather.3.cloned.1.call-done, bf16[16,9,64,128]{3,2,1,0:T(8,128)(2,1)} %bitcast.175, pred[16,9]{1,0:T(8,128)(4,1)S(1)} %copy.40), kind=kOutput, calls=%fused_computation.32 | convolution fusion | flops 303300608 | bytes 7340176 | tf_op jit(solution)/shard_map/hrkb,rkab->hra/dot_general | solution.py:71
  249.9 18.4 %all_to_all.75 = bf16[64,16,1,128]{3,0,2,1:T(8,128)(2,1)S(1)} all-to-all(bf16[64,16,1,128]{3,0,2,1:T(8,128)(2,1)S(1)} %fusion.42), channel_id=1, replica_groups=mesh['region_0'=4,'region_1'=8,'tm_0'=8,'tm_1'=2] {'tm_0','tm_1'}, dimensions={1} | all-to-all | bytes 524288 | tf_op jit(solution)/shard_map/all_to_all | solution.py:75
  268.3 0.8 fusion.35
  269.1 0.8 reduce.2
  270.1 14.5 %all_to_all.76 = bf16[16,2,4096]{2,1,0:T(2,128)(2,1)S(1)} all-to-all(bf16[16,2,4096]{2,1,0:T(2,128)(2,1)S(1)} %reshape.140), channel_id=1, replica_groups=mesh['region_0'=4,'region_1'=8,'tm_0'=8,'tm_1'=2] {'tm_0','tm_1'}, dimensions={0} | all-to-all | bytes 524288 | tf_op jit(solution)/shard_map/all_to_all | solution.py:76
  285.3 1.0 multiply_reduce_fusion
  286.4 6.7 %psum.136 = f32[]{:T(128)} all-reduce(f32[]{:T(128)} %multiply_reduce_fusion), channel_id=1, replica_groups=mesh['region_0'=4,'region_1'=8,'tm_0'=8,'tm_1'=2] {'region_0'}, use_global_device_ids=true, to_apply=%region_16.18 | all-reduce | flops 1 | bytes 8 | tf_op jit(solution)/shard_map/psum | solution.py:34
  293.1 17.2 %psum.137 = f32[]{:T(128)} all-reduce(f32[]{:T(128)} %psum.136), channel_id=1, replica_groups=mesh['region_0'=4,'region_1'=8,'tm_0'=8,'tm_1'=2] {'region_1'}, use_global_device_ids=true, to_apply=%region_17.19 | all-reduce | flops 1 | bytes 8 | tf_op jit(solution)/shard_map/psum | solution.py:34
  310.3 11.6 %psum.138 = f32[]{:T(128)} all-reduce(f32[]{:T(128)} %psum.137), channel_id=1, replica_groups=mesh['region_0'=4,'region_1'=8,'tm_0'=8,'tm_1'=2] {'tm_0'}, use_global_device_ids=true, to_apply=%region_18.20 | all-reduce | flops 1 | bytes 8 | tf_op jit(solution)/shard_map/psum | solution.py:34
  321.9 11.5 %psum.139 = f32[]{:T(128)} all-reduce(f32[]{:T(128)} %psum.138), channel_id=1, replica_groups=mesh['region_0'=4,'region_1'=8,'tm_0'=8,'tm_1'=2] {'tm_1'}, use_global_device_ids=true, to_apply=%region_19.21 | all-reduce | flops 1 | bytes 8 | tf_op jit(solution)/shard_map/psum | solution.py:34
  334.1 1.5 multiply_subtract_fusion
  (49 shorter events, 4.0 us)
Async XLA Ops:
  7.2 53.3 %all-gather.3.cloned.1.call-start = ((), (), s32[]{:S(2)}) async-start(), calls=%async_computation.6 | async-start | bytes 5013504 | tf_op jit(solution)/shard_map/all_gather | solution.py:53
  7.9 94.4 %all-gather.5.cloned.1.call-start = ((), (), s32[]{:S(2)}) async-start(), calls=%async_computation.7 | async-start | bytes 2359296 | tf_op jit(solution)/shard_map/all_gather | solution.py:28
  19.3 11.2 %collective-permute-start = (bf16[64,1024]{1,0:T(8,128)(2,1)S(1)}, bf16[64,1024]{1,0:T(8,128)(2,1)S(1)}, u32[]{:S(2)}, u32[]{:S(2)}) collective-permute-start(bf16[64,1024]{1,0:T(8,128)(2,1)S(1)} %get-tuple-element.26), channel_id=1, source_target_pairs={{0,16},{16,32},{32,48},{48,64},{64,80},{80,96},{96,112},{112,128},... | collective-permute-start | bytes 393224 | tf_op jit(solution)/shard_map/ppermute | solution.py:20
  21.2 10.2 %collective-permute-start.1 = (bf16[64,1024]{1,0:T(8,128)(2,1)S(1)}, bf16[64,1024]{1,0:T(8,128)(2,1)S(1)}, u32[]{:S(2)}, u32[]{:S(2)}) collective-permute-start(bf16[64,1024]{1,0:T(8,128)(2,1)S(1)} %get-tuple-element.27), channel_id=1, source_target_pairs={{16,0},{32,16},{48,32},{64,48},{80,64},{96,80},{112,96},{128,112},... | collective-permute-start | bytes 393224 | tf_op jit(solution)/shard_map/ppermute | solution.py:21
  65.5 36.9 %all-to-all-start = ((bf16[64,16,1,128]{3,0,2,1:T(8,128)(2,1)}), bf16[64,16,1,128]{3,0,2,1:T(8,128)(2,1)S(1)}, u32[]{:S(2)}, u32[]{:S(2)}) async-start(bf16[64,16,1,128]{3,0,2,1:T(8,128)(2,1)} %fusion.36), calls=%async_computation | async-start | bytes 524288 | tf_op jit(solution)/shard_map/all_to_all | solution.py:75
  106.2 20.8 %copy-start.3 = (f32[64,2048]{1,0:T(8,128)S(1)}, f32[64,2048]{1,0:T(8,128)}, u32[]{:S(2)}) copy-start(f32[64,2048]{1,0:T(8,128)} %param.8) | copy-start | bytes 1572868
  106.2 20.8 %copy-start.5 = (f32[64,2048]{1,0:T(8,128)S(1)}, f32[64,2048]{1,0:T(8,128)}, u32[]{:S(2)}) copy-start(f32[64,2048]{1,0:T(8,128)} %param.7) | copy-start | bytes 1572868
  127.3 11.4 %collective-permute-start.2 = (bf16[64,1024]{1,0:T(8,128)(2,1)S(1)}, bf16[64,1024]{1,0:T(8,128)(2,1)S(1)}, u32[]{:S(2)}, u32[]{:S(2)}) collective-permute-start(bf16[64,1024]{1,0:T(8,128)(2,1)S(1)} %get-tuple-element.24), channel_id=1, source_target_pairs={{0,16},{16,32},{32,48},{48,64},{64,80},{80,96},{96,112},{112,128},... | collective-permute-start | bytes 393224 | tf_op jit(solution)/shard_map/ppermute | solution.py:20
  130.6 9.5 %collective-permute-start.3 = (bf16[64,1024]{1,0:T(8,128)(2,1)S(1)}, bf16[64,1024]{1,0:T(8,128)(2,1)S(1)}, u32[]{:S(2)}, u32[]{:S(2)}) collective-permute-start(bf16[64,1024]{1,0:T(8,128)(2,1)S(1)} %get-tuple-element.25), channel_id=1, source_target_pairs={{16,0},{32,16},{48,32},{64,48},{80,64},{96,80},{112,96},{128,112},... | collective-permute-start | bytes 393224 | tf_op jit(solution)/shard_map/ppermute | solution.py:21
  142.7 19.8 %copy-start = (bf16[1024,1024]{1,0:T(8,128)(2,1)S(1)}, bf16[1024,1024]{1,0:T(8,128)(2,1)}, u32[]{:S(2)}) copy-start(bf16[1024,1024]{1,0:T(8,128)(2,1)} %all-gather.5.cloned.1.call-done) | copy-start | bytes 6291460
  179.4 62.0 %copy-start.1 = (f32[64,16,1,1,128]{4,1,0,3,2:T(8,128)}, f32[64,16,1,1,128]{4,1,0,3,2:T(8,128)S(1)}, u32[]{:S(2)}) copy-start(f32[64,16,1,1,128]{4,1,0,3,2:T(8,128)S(1)} %copy.53) | copy-start | bytes 1572868
  231.4 9.9 %collective-permute-start.4 = (bf16[64,1024]{1,0:T(8,128)(2,1)S(1)}, bf16[64,1024]{1,0:T(8,128)(2,1)S(1)}, u32[]{:S(2)}, u32[]{:S(2)}) collective-permute-start(bf16[64,1024]{1,0:T(8,128)(2,1)S(1)} %get-tuple-element.22), channel_id=1, source_target_pairs={{0,16},{16,32},{32,48},{48,64},{64,80},{80,96},{96,112},{112,128},... | collective-permute-start | bytes 393224 | tf_op jit(solution)/shard_map/ppermute | solution.py:20
  233.3 8.9 %collective-permute-start.5 = (bf16[64,1024]{1,0:T(8,128)(2,1)S(1)}, bf16[64,1024]{1,0:T(8,128)(2,1)S(1)}, u32[]{:S(2)}, u32[]{:S(2)}) collective-permute-start(bf16[64,1024]{1,0:T(8,128)(2,1)S(1)} %get-tuple-element.23), channel_id=1, source_target_pairs={{16,0},{32,16},{48,32},{64,48},{80,64},{96,80},{112,96},{128,112},... | collective-permute-start | bytes 393224 | tf_op jit(solution)/shard_map/ppermute | solution.py:21
  270.1 15.3 %copy-start.2 = (f32[64,16,1,1,128]{4,1,0,3,2:T(8,128)S(1)}, f32[64,16,1,1,128]{4,1,0,3,2:T(8,128)}, u32[]{:S(2)}) copy-start(f32[64,16,1,1,128]{4,1,0,3,2:T(8,128)} %copy-done.1) | copy-start | bytes 1572868
  284.6 49.4 %copy-start.4 = (f32[64,2048]{1,0:T(8,128)S(1)}, f32[64,2048]{1,0:T(8,128)}, u32[]{:S(2)}) copy-start(f32[64,2048]{1,0:T(8,128)} %param.8) | copy-start | bytes 1572868
Sparse Core Ops, SparseCore 0:
  10.1 50.3 all-gather.2
  62.5 39.7 all-gather.4
where the time goes:
time: 343 us; the launch traced here: 342 us
  blocking collectives  186 us (54%)
  waiting for transfers between devices  67.4 us (20%)
  starting transfers between devices  32.7 us (10%)
  matrix products  19.2 us (6%)
  between operations  18.8 us (5%)
  local copies, waits for them, and re-layouts  9.38 us (3%)
  other arithmetic  8.5 us (2%)
    psum x8, blocking collectives, one_axis_at_a_time(): value = lax.psum(value, axis)  94.3 us
    all_to_all x3, blocking collectives, operate(): lax.all_to_all(blended, TM, split_axis=0, concat_axis=1, tiled=True)  48.7 us
    all_to_all x2, blocking collectives, operate(): lax.all_to_all(spatial, TM, split_axis=1, concat_axis=0, tiled=True)  33.1 us
    all_gather x1, waiting for transfers between devices, gather_axes(): value = lax.all_gather(value, axis, axis=dim, tiled=True)  31.9 us
    all_gather x1, waiting for transfers between devices, local(): region_blocks = lax.all_gather(blocks, TM, axis=0, tiled=True)  27.8 us
    ppermute x3, starting transfers between devices, with_halo(): after = lax.ppermute(initial, axis, down)  20.6 us
    dot_general x3, matrix products, operate(): jnp.einsum('hrkb,rkab->hra', tile_stack, region_blocks, preferred_element...  15.1 us
    all_gather x1, blocking collectives, gather_axes(): value = lax.all_gather(value, axis, axis=dim, tiled=True)  10.2 us
  transfers between devices with their start and end apart: 9, of which 8 were waited for; matrix products, arithmetic and copies ran while one was open for 2% of the time, Pallas kernels for 0%

commit v1 on v0

--- a/solution.py
+++ b/solution.py
@@ -31,7 +31,7 @@
 
 def one_axis_at_a_time(value, axes):
     for axis in axes:
-        value = lax.psum(value, axis)
+        value = jnp.sum(lax.all_gather(value, axis), axis=0)
     return value
 
 

time: 343 us -> 374 us (1.090)
  local copies, waits for them, and re-layouts: 9.38 us -> 36.7 us
  blocking collectives: 186 us -> 167 us
  other arithmetic: 8.5 us -> 18.3 us
  waiting for transfers between devices: 67.4 us -> 76.9 us
    psum x8 -> x0, blocking collectives: 94.3 us -> none  [one_axis_at_a_time(): value = lax.psum(value, axis)]
    unnamed x0 -> x8, blocking collectives: none -> 89.3 us
    unnamed x21 -> x57, local copies, waits for them, and re-layouts: 1.53 us -> 28.8 us
    all_to_all x3 -> x2, blocking collectives: 48.7 us -> 34.5 us  [operate(): lax.all_to_all(blended, TM, split_axis=0, concat_axis=1, tiled=True)]
    reduce_sum x0 -> x16, other arithmetic: none -> 9.74 us  [one_axis_at_a_time(): value = jnp.sum(lax.all_gather(value, axis), axis=0)]
    all_to_all x0 -> x1, waiting for transfers between devices: none -> 9.63 us  [operate(): lax.all_to_all(blended, TM, split_axis=0, concat_axis=1, tiled=True)]
  transfers between devices with their start and end apart: 9 -> 10, of which waited for: 8 -> 9; matrix products, arithmetic and copies ran while one was open for 2% -> 3% of each run, Pallas kernels for 0% -> 0%
where the time goes in v1:
time: 374 us; the launch traced here: 373 us
  blocking collectives  167 us (45%)
  waiting for transfers between devices  76.9 us (21%)
  local copies, waits for them, and re-layouts  36.7 us (10%)
  starting transfers between devices  36.4 us (10%)
  matrix products  19.2 us (5%)
  between operations  18.8 us (5%)
  other arithmetic  18.3 us (5%)
    unnamed x8, blocking collectives  89.3 us
    all_to_all x2, blocking collectives, operate(): lax.all_to_all(blended, TM, split_axis=0, concat_axis=1, tiled=True)  34.5 us
    all_to_all x2, blocking collectives, operate(): lax.all_to_all(spatial, TM, split_axis=1, concat_axis=0, tiled=True)  32.8 us
    all_gather x1, waiting for transfers between devices, gather_axes(): value = lax.all_gather(value, axis, axis=dim, tiled=True)  31.9 us
    unnamed x57, local copies, waits for them, and re-layouts  28.8 us
    all_gather x1, waiting for transfers between devices, local(): region_blocks = lax.all_gather(blocks, TM, axis=0, tiled=True)  27.8 us
    ppermute x3, starting transfers between devices, with_halo(): after = lax.ppermute(initial, axis, down)  20.7 us
    dot_general x3, matrix products, operate(): jnp.einsum('hrkb,rkab->hra', tile_stack, region_blocks, preferred_element...  15.1 us
  transfers between devices with their start and end apart: 10, of which 9 were waited for; matrix products, arithmetic and copies ran while one was open for 3% of the time, Pallas kernels for 0%

profile of v1, /device:TPU:1, one launch (start us, length us, event | category | flops | bytes accessed | tf_op | source)
XLA Modules:
  0.0 373.0 jit_solution(5235077481978897174)
XLA Ops:
  7.9 10.2 %all_gather.114 = bf16[128,1024]{1,0:T(8,128)(2,1)} all-gather(bf16[64,1024]{1,0:T(8,128)(2,1)} %param.11), channel_id=1, replica_groups=mesh['region_0'=4,'region_1'=8,'tm_0'=8,'tm_1'=2] {'tm_1'}, dimensions={0}, use_global_device_ids=true | all-gather | bytes 393216 | tf_op jit(solution)/shard_map/all_gather | solution.py:28
  19.3 1.9 collective-permute-start
  21.2 7.5 %collective-permute-start.1 = (bf16[64,1024]{1,0:T(8,128)(2,1)S(1)}, bf16[64,1024]{1,0:T(8,128)(2,1)S(1)}, u32[]{:S(2)}, u32[]{:S(2)}) collective-permute-start(bf16[64,1024]{1,0:T(8,128)(2,1)S(1)} %get-tuple-element.27), channel_id=1, source_target_pairs={{16,0},{32,16},{48,32},{64,48},{80,64},{96,80},{112,96},{128,112},... | collective-permute-start | bytes 393224 | tf_op jit(solution)/shard_map/ppermute | solution.py:21
  32.6 27.8 %all-gather.3.cloned.1.call-done = bf16[16,9,128,128]{3,2,1,0:T(8,128)(2,1)} async-done(((bf16[1,9,128,128]{3,2,1,0:T(8,128)(2,1)}), bf16[16,9,128,128]{3,2,1,0:T(8,128)(2,1)}) %all-gather.3.cloned.1.call-update) | async-done | bytes 4718608 | tf_op jit(solution)/shard_map/all_gather | solution.py:53
  60.5 5.0 %fusion.36 = bf16[64,16,1,128]{3,0,2,1:T(8,128)(2,1)} fusion(bf16[16,9,128,128]{3,2,1,0:T(8,128)(2,1)} %all-gather.3.cloned.1.call-done, bf16[16,9,64,128]{3,2,1,0:T(8,128)(2,1)S(1)} %bitcast.194, pred[16,9]{1,0:T(8,128)(4,1)S(1)} %copy.40), kind=kOutput, calls=%fused_computation.30 | convolution fusion | flops 303300608 | bytes 7340176 | tf_op jit(solution)/shard_map/hrkb,rkab->hra/dot_general | solution.py:71
  65.4 5.0 %all-to-all-start = ((bf16[64,16,1,128]{3,0,2,1:T(8,128)(2,1)}), bf16[64,16,1,128]{3,0,2,1:T(8,128)(2,1)S(1)}, u32[]{:S(2)}, u32[]{:S(2)}) async-start(bf16[64,16,1,128]{3,0,2,1:T(8,128)(2,1)} %fusion.36), calls=%async_computation | async-start | bytes 524288 | tf_op jit(solution)/shard_map/all_to_all | solution.py:75
  70.4 31.9 %all-gather.5.cloned.1.call-done = bf16[1024,1024]{1,0:T(8,128)(2,1)} async-done(((bf16[128,1024]{1,0:T(8,128)(2,1)}), bf16[1024,1024]{1,0:T(8,128)(2,1)}) %all-gather.5.cloned.1.call-update) | async-done | bytes 2097168 | tf_op jit(solution)/shard_map/all_gather | solution.py:28
  102.3 2.4 fusion.33
  106.3 20.0 %all_to_all.72 = bf16[16,2,4096]{2,1,0:T(2,128)(2,1)S(1)} all-to-all(bf16[16,2,4096]{2,1,0:T(2,128)(2,1)S(1)} %reshape.216), channel_id=1, replica_groups=mesh['region_0'=4,'region_1'=8,'tm_0'=8,'tm_1'=2] {'tm_0','tm_1'}, dimensions={0} | all-to-all | bytes 524288 | tf_op jit(solution)/shard_map/all_to_all | solution.py:76
  127.3 3.3 collective-permute-start.2
  130.6 6.4 %collective-permute-start.3 = (bf16[64,1024]{1,0:T(8,128)(2,1)S(1)}, bf16[64,1024]{1,0:T(8,128)(2,1)S(1)}, u32[]{:S(2)}, u32[]{:S(2)}) collective-permute-start(bf16[64,1024]{1,0:T(8,128)(2,1)S(1)} %get-tuple-element.25), channel_id=1, source_target_pairs={{16,0},{32,16},{48,32},{64,48},{80,64},{96,80},{112,96},{128,112},... | collective-permute-start | bytes 393224 | tf_op jit(solution)/shard_map/ppermute | solution.py:21
  136.9 1.8 collective-permute-done.2
  138.7 1.4 collective-permute-done.3
  140.2 2.5 gather_fusion.1
  142.7 5.1 %fusion.39 = bf16[64,16,1,128]{3,0,2,1:T(8,128)(2,1)S(1)} fusion(bf16[16,9,128,128]{3,2,1,0:T(8,128)(2,1)} %all-gather.3.cloned.1.call-done, bf16[16,9,64,128]{3,2,1,0:T(8,128)(2,1)} %bitcast.196, pred[16,9]{1,0:T(8,128)(4,1)S(1)} %copy.40), kind=kOutput, calls=%fused_computation.31 | convolution fusion | flops 303300608 | bytes 7340176 | tf_op jit(solution)/shard_map/hrkb,rkab->hra/dot_general | solution.py:71
  147.9 14.7 %all_to_all.73 = bf16[64,16,1,128]{3,0,2,1:T(8,128)(2,1)S(1)} all-to-all(bf16[64,16,1,128]{3,0,2,1:T(8,128)(2,1)S(1)} %fusion.39), channel_id=1, replica_groups=mesh['region_0'=4,'region_1'=8,'tm_0'=8,'tm_1'=2] {'tm_0','tm_1'}, dimensions={1} | all-to-all | bytes 524288 | tf_op jit(solution)/shard_map/all_to_all | solution.py:75
  165.1 3.4 all-to-all-start.3
  168.6 1.3 dynamic-slice
  169.9 9.6 %all-to-all-done.3 = bf16[16,2,4096]{2,1,0:T(2,128)(2,1)S(1)} async-done(((bf16[16,2,4096]{2,1,0:T(2,128)(2,1)}), bf16[16,2,4096]{2,1,0:T(2,128)(2,1)S(1)}, u32[]{:S(2)}, u32[]{:S(2)}) %all-to-all-start.3) | async-done | bytes 262176 | tf_op jit(solution)/shard_map/all_to_all | solution.py:76
  181.1 1.4 dynamic-update-slice.4
  182.5 1.3 dynamic-update-slice.8
  183.8 1.4 dynamic-update-slice
  185.2 1.3 dynamic-slice.1
  186.5 6.5 %all-reduce.18 = (f32[4]{0:T(128)S(1)}, f32[4]{0:T(128)S(1)}, f32[4]{0:T(128)S(1)}) all-reduce(f32[4]{0:T(128)S(1)} %dynamic-update-slice, f32[4]{0:T(128)S(1)} %dynamic-update-slice.4, f32[4]{0:T(128)S(1)} %dynamic-update-slice.8), channel_id=1, replica_groups=mesh['region_0'=4,'region_1'=8,'tm_0'=8,'tm_1'=2] {'region_0'}, use_global_device_ids=true, to_apply=%add | all-reduce | flops 12 | bytes 96
  194.3 1.3 dynamic-update-slice.9
  200.0 15.9 %all-reduce.17 = (f32[8]{0:T(128)S(1)}, f32[8]{0:T(128)S(1)}, f32[8]{0:T(128)S(1)}) all-reduce(f32[8]{0:T(128)S(1)} %dynamic-update-slice.1, f32[8]{0:T(128)S(1)} %dynamic-update-slice.5, f32[8]{0:T(128)S(1)} %dynamic-update-slice.9), channel_id=1, replica_groups=mesh['region_0'=4,'region_1'=8,'tm_0'=8,'tm_1'=2] {'region_1'}, use_global_device_ids=true, to_apply=%add.1 | all-reduce | flops 24 | bytes 192
  217.1 1.3 dynamic-update-slice.10
  221.5 1.3 dynamic-slice.3
  222.8 10.7 %all-reduce.16 = (f32[8]{0:T(128)S(1)}, f32[8]{0:T(128)S(1)}, f32[8]{0:T(128)S(1)}) all-reduce(f32[8]{0:T(128)S(1)} %dynamic-update-slice.2, f32[8]{0:T(128)S(1)} %dynamic-update-slice.6, f32[8]{0:T(128)S(1)} %dynamic-update-slice.10), channel_id=1, replica_groups=mesh['region_0'=4,'region_1'=8,'tm_0'=8,'tm_1'=2] {'tm_0'}, use_global_device_ids=true, to_apply=%add.2 | all-reduce | flops 24 | bytes 192
  234.7 1.4 dynamic-update-slice.11
  236.1 1.3 dynamic-update-slice.7
  238.1 1.3 dynamic-update-slice.3
  239.4 11.7 %all-reduce.19 = (f32[2]{0:T(128)S(1)}, f32[2]{0:T(128)S(1)}, f32[2]{0:T(128)S(1)}) all-reduce(f32[2]{0:T(128)S(1)} %dynamic-update-slice.3, f32[2]{0:T(128)S(1)} %dynamic-update-slice.7, f32[2]{0:T(128)S(1)} %dynamic-update-slice.11), channel_id=1, replica_groups=mesh['region_0'=4,'region_1'=8,'tm_0'=8,'tm_1'=2] {'tm_1'}, use_global_device_ids=true, to_apply=%add.3 | all-reduce | flops 6 | bytes 48
  256.9 1.9 collective-permute-start.4
  258.8 6.9 %collective-permute-start.5 = (bf16[64,1024]{1,0:T(8,128)(2,1)S(1)}, bf16[64,1024]{1,0:T(8,128)(2,1)S(1)}, u32[]{:S(2)}, u32[]{:S(2)}) collective-permute-start(bf16[64,1024]{1,0:T(8,128)(2,1)S(1)} %get-tuple-element.23), channel_id=1, source_target_pairs={{16,0},{32,16},{48,32},{64,48},{80,64},{96,80},{112,96},{128,112},... | collective-permute-start | bytes 393224 | tf_op jit(solution)/shard_map/ppermute | solution.py:21
  267.9 2.5 gather_fusion.2
  270.4 5.0 %fusion.42 = bf16[64,16,1,128]{3,0,2,1:T(8,128)(2,1)S(1)} fusion(bf16[16,9,128,128]{3,2,1,0:T(8,128)(2,1)} %all-gather.3.cloned.1.call-done, bf16[16,9,64,128]{3,2,1,0:T(8,128)(2,1)} %bitcast.195, pred[16,9]{1,0:T(8,128)(4,1)S(1)} %copy.40), kind=kOutput, calls=%fused_computation.32 | convolution fusion | flops 303300608 | bytes 7340176 | tf_op jit(solution)/shard_map/hrkb,rkab->hra/dot_general | solution.py:71
  275.4 18.1 %all_to_all.74 = bf16[64,16,1,128]{3,0,2,1:T(8,128)(2,1)S(1)} all-to-all(bf16[64,16,1,128]{3,0,2,1:T(8,128)(2,1)S(1)} %fusion.42), channel_id=1, replica_groups=mesh['region_0'=4,'region_1'=8,'tm_0'=8,'tm_1'=2] {'tm_0','tm_1'}, dimensions={1} | all-to-all | bytes 524288 | tf_op jit(solution)/shard_map/all_to_all | solution.py:75
  295.4 14.5 %all_to_all.75 = bf16[16,2,4096]{2,1,0:T(2,128)(2,1)S(1)} all-to-all(bf16[16,2,4096]{2,1,0:T(2,128)(2,1)S(1)} %reshape.220), channel_id=1, replica_groups=mesh['region_0'=4,'region_1'=8,'tm_0'=8,'tm_1'=2] {'tm_0','tm_1'}, dimensions={0} | all-to-all | bytes 524288 | tf_op jit(solution)/shard_map/all_to_all | solution.py:76
  311.6 1.4 dynamic-update-slice.12
  313.0 6.1 %all-reduce.12 = f32[4]{0:T(128)S(1)} all-reduce(f32[4]{0:T(128)S(1)} %dynamic-update-slice.12), channel_id=1, replica_groups=mesh['region_0'=4,'region_1'=8,'tm_0'=8,'tm_1'=2] {'region_0'}, use_global_device_ids=true, to_apply=%add.12 | all-reduce | flops 4 | bytes 32
  319.7 1.4 dynamic-update-slice.13
  321.0 16.5 %all-reduce.13 = f32[8]{0:T(128)S(1)} all-reduce(f32[8]{0:T(128)S(1)} %dynamic-update-slice.13), channel_id=1, replica_groups=mesh['region_0'=4,'region_1'=8,'tm_0'=8,'tm_1'=2] {'region_1'}, use_global_device_ids=true, to_apply=%add.13 | all-reduce | flops 8 | bytes 64
  338.2 1.3 dynamic-update-slice.14
  339.5 11.0 %all-reduce.14 = f32[8]{0:T(128)S(1)} all-reduce(f32[8]{0:T(128)S(1)} %dynamic-update-slice.14), channel_id=1, replica_groups=mesh['region_0'=4,'region_1'=8,'tm_0'=8,'tm_1'=2] {'tm_0'}, use_global_device_ids=true, to_apply=%add.14 | all-reduce | flops 8 | bytes 64
  351.1 1.4 dynamic-update-slice.15
  352.6 10.8 %all-reduce.15 = f32[2]{0:T(128)S(1)} all-reduce(f32[2]{0:T(128)S(1)} %dynamic-update-slice.15), channel_id=1, replica_groups=mesh['region_0'=4,'region_1'=8,'tm_0'=8,'tm_1'=2] {'tm_1'}, use_global_device_ids=true, to_apply=%add.15 | all-reduce | flops 2 | bytes 16
  364.7 1.5 multiply_subtract_fusion
  (102 shorter events, 34.4 us)
Async XLA Ops:
  7.2 53.3 %all-gather.3.cloned.1.call-start = ((), (), s32[]{:S(2)}) async-start(), calls=%async_computation.6 | async-start | bytes 5013504 | tf_op jit(solution)/shard_map/all_gather | solution.py:53
  7.9 94.4 %all-gather.5.cloned.1.call-start = ((), (), s32[]{:S(2)}) async-start(), calls=%async_computation.7 | async-start | bytes 2359296 | tf_op jit(solution)/shard_map/all_gather | solution.py:28
  19.3 11.2 %collective-permute-start = (bf16[64,1024]{1,0:T(8,128)(2,1)S(1)}, bf16[64,1024]{1,0:T(8,128)(2,1)S(1)}, u32[]{:S(2)}, u32[]{:S(2)}) collective-permute-start(bf16[64,1024]{1,0:T(8,128)(2,1)S(1)} %get-tuple-element.26), channel_id=1, source_target_pairs={{0,16},{16,32},{32,48},{48,64},{64,80},{80,96},{96,112},{112,128},... | collective-permute-start | bytes 393224 | tf_op jit(solution)/shard_map/ppermute | solution.py:20
  21.2 10.2 %collective-permute-start.1 = (bf16[64,1024]{1,0:T(8,128)(2,1)S(1)}, bf16[64,1024]{1,0:T(8,128)(2,1)S(1)}, u32[]{:S(2)}, u32[]{:S(2)}) collective-permute-start(bf16[64,1024]{1,0:T(8,128)(2,1)S(1)} %get-tuple-element.27), channel_id=1, source_target_pairs={{16,0},{32,16},{48,32},{64,48},{80,64},{96,80},{112,96},{128,112},... | collective-permute-start | bytes 393224 | tf_op jit(solution)/shard_map/ppermute | solution.py:21
  65.4 36.9 %all-to-all-start = ((bf16[64,16,1,128]{3,0,2,1:T(8,128)(2,1)}), bf16[64,16,1,128]{3,0,2,1:T(8,128)(2,1)S(1)}, u32[]{:S(2)}, u32[]{:S(2)}) async-start(bf16[64,16,1,128]{3,0,2,1:T(8,128)(2,1)} %fusion.36), calls=%async_computation | async-start | bytes 524288 | tf_op jit(solution)/shard_map/all_to_all | solution.py:75
  106.2 20.8 %copy-start.3 = (f32[64,2048]{1,0:T(8,128)S(1)}, f32[64,2048]{1,0:T(8,128)}, u32[]{:S(2)}) copy-start(f32[64,2048]{1,0:T(8,128)} %param.8) | copy-start | bytes 1572868
  106.2 20.8 %copy-start.5 = (f32[64,2048]{1,0:T(8,128)S(1)}, f32[64,2048]{1,0:T(8,128)}, u32[]{:S(2)}) copy-start(f32[64,2048]{1,0:T(8,128)} %param.7) | copy-start | bytes 1572868
  127.3 11.4 %collective-permute-start.2 = (bf16[64,1024]{1,0:T(8,128)(2,1)S(1)}, bf16[64,1024]{1,0:T(8,128)(2,1)S(1)}, u32[]{:S(2)}, u32[]{:S(2)}) collective-permute-start(bf16[64,1024]{1,0:T(8,128)(2,1)S(1)} %get-tuple-element.24), channel_id=1, source_target_pairs={{0,16},{16,32},{32,48},{48,64},{64,80},{80,96},{96,112},{112,128},... | collective-permute-start | bytes 393224 | tf_op jit(solution)/shard_map/ppermute | solution.py:20
  130.6 9.5 %collective-permute-start.3 = (bf16[64,1024]{1,0:T(8,128)(2,1)S(1)}, bf16[64,1024]{1,0:T(8,128)(2,1)S(1)}, u32[]{:S(2)}, u32[]{:S(2)}) collective-permute-start(bf16[64,1024]{1,0:T(8,128)(2,1)S(1)} %get-tuple-element.25), channel_id=1, source_target_pairs={{16,0},{32,16},{48,32},{64,48},{80,64},{96,80},{112,96},{128,112},... | collective-permute-start | bytes 393224 | tf_op jit(solution)/shard_map/ppermute | solution.py:21
  142.7 19.8 %copy-start = (bf16[1024,1024]{1,0:T(8,128)(2,1)S(1)}, bf16[1024,1024]{1,0:T(8,128)(2,1)}, u32[]{:S(2)}) copy-start(bf16[1024,1024]{1,0:T(8,128)(2,1)} %all-gather.5.cloned.1.call-done) | copy-start | bytes 6291460
  165.1 14.4 %all-to-all-start.3 = ((bf16[16,2,4096]{2,1,0:T(2,128)(2,1)}), bf16[16,2,4096]{2,1,0:T(2,128)(2,1)S(1)}, u32[]{:S(2)}, u32[]{:S(2)}) async-start(bf16[16,2,4096]{2,1,0:T(2,128)(2,1)} %reshape.218), calls=%async_computation.3 | async-start | bytes 524288 | tf_op jit(solution)/shard_map/all_to_all | solution.py:76
  180.2 86.6 %copy-start.1 = (f32[64,16,1,1,128]{4,1,0,3,2:T(8,128)}, f32[64,16,1,1,128]{4,1,0,3,2:T(8,128)S(1)}, u32[]{:S(2)}) copy-start(f32[64,16,1,1,128]{4,1,0,3,2:T(8,128)S(1)} %copy.53) | copy-start | bytes 1572868
  256.9 9.9 %collective-permute-start.4 = (bf16[64,1024]{1,0:T(8,128)(2,1)S(1)}, bf16[64,1024]{1,0:T(8,128)(2,1)S(1)}, u32[]{:S(2)}, u32[]{:S(2)}) collective-permute-start(bf16[64,1024]{1,0:T(8,128)(2,1)S(1)} %get-tuple-element.22), channel_id=1, source_target_pairs={{0,16},{16,32},{32,48},{48,64},{64,80},{80,96},{96,112},{112,128},... | collective-permute-start | bytes 393224 | tf_op jit(solution)/shard_map/ppermute | solution.py:20
  258.8 8.9 %collective-permute-start.5 = (bf16[64,1024]{1,0:T(8,128)(2,1)S(1)}, bf16[64,1024]{1,0:T(8,128)(2,1)S(1)}, u32[]{:S(2)}, u32[]{:S(2)}) collective-permute-start(bf16[64,1024]{1,0:T(8,128)(2,1)S(1)} %get-tuple-element.23), channel_id=1, source_target_pairs={{16,0},{32,16},{48,32},{64,48},{80,64},{96,80},{112,96},{128,112},... | collective-permute-start | bytes 393224 | tf_op jit(solution)/shard_map/ppermute | solution.py:21
  295.3 15.3 %copy-start.2 = (f32[64,16,1,1,128]{4,1,0,3,2:T(8,128)S(1)}, f32[64,16,1,1,128]{4,1,0,3,2:T(8,128)}, u32[]{:S(2)}) copy-start(f32[64,16,1,1,128]{4,1,0,3,2:T(8,128)} %copy-done.1) | copy-start | bytes 1572868
  309.9 54.8 %copy-start.4 = (f32[64,2048]{1,0:T(8,128)S(1)}, f32[64,2048]{1,0:T(8,128)}, u32[]{:S(2)}) copy-start(f32[64,2048]{1,0:T(8,128)} %param.8) | copy-start | bytes 1572868
Sparse Core Ops, SparseCore 0:
  10.1 50.3 all-gather.2
  62.5 39.7 all-gather.4
